TPU v7x, 32 devices: a whole 2x2x4 slice. The times are simulated.
32 devices in a mesh: group: 2 (over x), wide: 2 (over core), tensor: 8 (over z, y).
Axes of the slice: x: 2, y: 2, z: 4, core: 2. Of those that a mesh axis runs over, the one named last changes fastest.
Arguments:
- tokens: bfloat16 [512, 8192], P(('group', 'wide'), 'tensor'), parts along dimension 0, may hold values from -6 to 6
- gain: float32 [16384], P('group'), parts along dimension 0, may hold values from 0.5 to 2
- gate_weight: bfloat16 [16384, 16384], P(('group', 'wide', 'tensor')), parts along dimension 0, may hold values from -0.09375 to 0.09375
- up_weight: bfloat16 [16384, 16384], P(('group', 'wide', 'tensor')), parts along dimension 0, may hold values from -0.09375 to 0.09375
- gate_mask: int32 [256, 256], P('group'), parts along dimension 0, may hold values from 0 to 1, as said below
- up_mask: int32 [256, 256], P('group'), parts along dimension 0, may hold values from 0 to 1, as said below
Outputs:
- hidden: bfloat16 [512, 16384], P(('group', 'wide'), 'tensor'), parts along dimension 0
There are 2 independent parts, one for each index of `group`. A program takes and returns all parts, laid end to end along the dimension named above; each array names one. Nothing has to cross between parts.
Inputs may be any that keep to these rules, and one draw needn't show every extreme that they name: `gate_mask`: A 1 keeps a block, a 0 prunes it; the share of kept blocks differs between groups of consecutive hidden-unit blocks. `up_mask`: as for gate_mask.
All inputs are finite; a program needn't handle non-finite values.
Results may differ from a plain program's by a relative error of at most 0.0058.
Values may be sent and summed in bfloat16 or wider, within the bound.
A program may use at most 256 MiB of HBM per device.

v0:
```python
import jax
import jax.numpy as jnp
from jax import lax
from jax.sharding import PartitionSpec as P

D = 8192
FF = 16384
BS = 64


def apply_mask(weight, mask):
    rows, cols = mask.shape
    blocks = weight.reshape(rows, weight.shape[0] // rows, cols, weight.shape[1] // cols)
    blocks = blocks * mask.astype(jnp.bfloat16)[:, None, :, None]
    return blocks.reshape(weight.shape)


def local(tokens, gain, gate_weight, up_weight, gate_mask, up_mask):
    whole = lax.all_gather(tokens, "tensor", axis=1, tiled=True)
    values = whole.astype(jnp.float32)
    scale = lax.rsqrt(jnp.mean(values * values, axis=-1, keepdims=True) + 1e-05)
    normed = (values * scale * gain).astype(jnp.bfloat16)
    shard = lax.axis_index("tensor")
    half = lax.axis_index("wide")
    width = FF // lax.axis_size("tensor")
    half_rows = D // lax.axis_size("wide")
    col_blocks = width // BS
    row_blocks = half_rows // BS
    first_col = shard * col_blocks
    gate_half = lax.all_to_all(gate_weight, "tensor", split_axis=1, concat_axis=0, tiled=True)
    up_half = lax.all_to_all(up_weight, "tensor", split_axis=1, concat_axis=0, tiled=True)
    first_row = half * row_blocks
    gate_kept = apply_mask(
        gate_half, lax.dynamic_slice(gate_mask, (first_row, first_col), (row_blocks, col_blocks))
    )
    up_kept = apply_mask(
        up_half, lax.dynamic_slice(up_mask, (first_row, first_col), (row_blocks, col_blocks))
    )
    features_half = lax.all_to_all(normed, "wide", split_axis=1, concat_axis=0, tiled=True)
    gate_part = jnp.dot(features_half, gate_kept, preferred_element_type=jnp.float32)
    up_part = jnp.dot(features_half, up_kept, preferred_element_type=jnp.float32)
    gate, up = (
        lax.psum_scatter(gate_part, "wide", scatter_dimension=0, tiled=True),
        lax.psum_scatter(up_part, "wide", scatter_dimension=0, tiled=True),
    )
    return (jax.nn.silu(gate) * up).astype(jnp.bfloat16)


def solution(mesh):
    in_specs = (
        P(("group", "wide"), "tensor"),
        P("group"),
        P(("group", "wide", "tensor"), None),
        P(("group", "wide", "tensor"), None),
        P("group", None),
        P("group", None),
    )
    out_specs = P(("group", "wide"), "tensor")
    return jax.shard_map(local, mesh=mesh, in_specs=in_specs, out_specs=out_specs, check_vma=False)
```

profile of v0, /device:TPU:17, one launch (start us, length us, event | category | flops | bytes accessed | tf_op | source)
XLA Modules:
  0.0 876.9 jit_solution(4451933863547242540)
XLA Ops:
  6.5 1.8 copy.7
  8.3 0.0 all-gather.2.cloned.1.call-update
  8.4 22.4 %copy.9 = bf16[512,16384]{0,1:T(8,128)(2,1)} copy(bf16[512,16384]{1,0:T(8,128)(2,1)} %param.8) | data formatting | bytes 33554432 | tf_op args[2]
  30.8 27.6 %all-gather.2.cloned.1.call-done = bf16[128,8192]{0,1:T(8,128)(2,1)} async-done(((bf16[128,1024]{0,1:T(8,128)(2,1)}), bf16[128,8192]{0,1:T(8,128)(2,1)}) %all-gather.2.cloned.1.call-update) | async-done | bytes 2097168 | tf_op jit(solution)/shard_map/all_gather | solution.py:19
  58.4 2.7 fusion
  61.1 4.6 fusion.2
  65.7 6.4 all_to_all.51
  72.1 6.4 all-to-all-start.1
  78.5 22.5 %copy.12 = bf16[512,16384]{0,1:T(8,128)(2,1)} copy(bf16[512,16384]{1,0:T(8,128)(2,1)} %param.9) | data formatting | bytes 33554432 | tf_op args[3]
  101.0 337.1 %all-to-all-done.1 = bf16[512,8,2048]{0,2,1:T(8,128)(2,1)} async-done(((bf16[512,8,2048]{0,2,1:T(8,128)(2,1)}), bf16[512,8,2048]{0,2,1:T(8,128)(2,1)}, u32[]{:S(2)}, u32[]{:S(2)}) %all-to-all-start.1) | async-done | bytes 16777248 | tf_op jit(solution)/shard_map/all_to_all | solution.py:30
  438.1 8.7 all-to-all-start.2
  446.8 0.9 dynamic-slice_convert_fusion
  447.7 11.2 %mul.67 = bf16[64,64,32,64]{3,2,1,0:T(8,128)(2,1)} broadcast(bf16[64,32]{1,0:T(8,128)(2,1)S(1)} %get-tuple-element.6), dimensions={0,2} | broadcast | bytes 16781312 | tf_op jit(solution)/shard_map/mul | solution.py:14
  458.9 45.9 %mul.68 = bf16[8,512,2048]{2,1,0:T(8,128)(2,1)} reshape(bf16[64,64,32,64]{3,2,1,0:T(8,128)(2,1)} %mul.67) | data formatting | bytes 33554432 | tf_op jit(solution)/shard_map/mul | solution.py:14
  504.7 21.6 %copy.10 = bf16[8,512,2048]{1,2,0:T(8,128)(2,1)} copy(bf16[8,512,2048]{2,1,0:T(8,128)(2,1)} %mul.68) | data formatting | bytes 33554432 | tf_op jit(solution)/shard_map/mul | solution.py:14
  526.4 11.1 %mul.72 = bf16[64,64,32,64]{3,2,1,0:T(8,128)(2,1)} broadcast(bf16[64,32]{1,0:T(8,128)(2,1)S(1)} %get-tuple-element.5), dimensions={0,2} | broadcast | bytes 16781312 | tf_op jit(solution)/shard_map/mul | solution.py:14
  537.4 45.9 %mul.73 = bf16[8,512,2048]{2,1,0:T(8,128)(2,1)} reshape(bf16[64,64,32,64]{3,2,1,0:T(8,128)(2,1)} %mul.72) | data formatting | bytes 33554432 | tf_op jit(solution)/shard_map/mul | solution.py:14
  583.3 21.6 %copy.13 = bf16[8,512,2048]{1,2,0:T(8,128)(2,1)} copy(bf16[8,512,2048]{2,1,0:T(8,128)(2,1)} %mul.73) | data formatting | bytes 33554432 | tf_op jit(solution)/shard_map/mul | solution.py:14
  604.9 2.8 copy.8
  607.7 17.2 %bitcast_multiply_fusion.1 = bf16[8,512,2048]{1,2,0:T(8,128)(2,1)} fusion(bf16[8,512,2048]{1,2,0:T(8,128)(2,1)} %copy.10, bf16[512,8,2048]{0,2,1:T(8,128)(2,1)} %all-to-all-done.1), kind=kLoop, calls=%fused_computation.1 | loop fusion | flops 8388608 | bytes 50331648 | tf_op jit(solution)/shard_map/mul | solution.py:14
  624.9 21.8 %copy.11 = bf16[8,512,2048]{2,1,0:T(8,128)(2,1)} copy(bf16[8,512,2048]{1,2,0:T(8,128)(2,1)} %bitcast_multiply_fusion.1) | data formatting | bytes 33554432 | tf_op jit(solution)/shard_map/mul | solution.py:14
  646.7 9.4 %fusion.3 = f32[256,2048]{1,0:T(8,128)} fusion(bf16[256,4096]{1,0:T(8,128)(2,1)S(1)} %bitcast.25, bf16[4096,2048]{1,0:T(8,128)(2,1)} %bitcast.22), kind=kOutput, calls=%fused_computation.11 | convolution fusion | flops 4294967296 | bytes 20971520 | tf_op jit(solution)/shard_map/dot_general | solution.py:40
  656.1 0.0 reduce-scatter.3.cloned.1.call-update
  656.1 0.2 reduce-scatter.5.cloned.1.call-start
  656.4 149.2 %all-to-all-done.2 = bf16[512,8,2048]{0,2,1:T(8,128)(2,1)} async-done(((bf16[512,8,2048]{0,2,1:T(8,128)(2,1)}), bf16[512,8,2048]{0,2,1:T(8,128)(2,1)}, u32[]{:S(2)}, u32[]{:S(2)}) %all-to-all-start.2) | async-done | bytes 16777248 | tf_op jit(solution)/shard_map/all_to_all | solution.py:31
  805.6 17.2 %bitcast_multiply_fusion = bf16[8,512,2048]{1,2,0:T(8,128)(2,1)} fusion(bf16[8,512,2048]{1,2,0:T(8,128)(2,1)} %copy.13, bf16[512,8,2048]{0,2,1:T(8,128)(2,1)} %all-to-all-done.2), kind=kLoop, calls=%fused_computation | loop fusion | flops 8388608 | bytes 50331648 | tf_op jit(solution)/shard_map/mul | solution.py:14
  822.7 21.7 %copy.14 = bf16[8,512,2048]{2,1,0:T(8,128)(2,1)} copy(bf16[8,512,2048]{1,2,0:T(8,128)(2,1)} %bitcast_multiply_fusion) | data formatting | bytes 33554432 | tf_op jit(solution)/shard_map/mul | solution.py:14
  844.4 9.5 %fusion.4 = f32[256,2048]{1,0:T(8,128)} fusion(bf16[256,4096]{1,0:T(8,128)(2,1)S(1)} %bitcast.26, bf16[4096,2048]{1,0:T(8,128)(2,1)} %bitcast.21), kind=kOutput, calls=%fused_computation.12 | convolution fusion | flops 4294967296 | bytes 20971520 | tf_op jit(solution)/shard_map/dot_general | solution.py:41
  853.9 0.0 reduce-scatter.5.cloned.1.call-update
  853.9 0.0 reduce-scatter.3.cloned.1.call-done
  853.9 13.8 %reduce-scatter.5.cloned.1.call-done = f32[128,2048]{1,0:T(8,128)} async-done(((f32[256,2048]{1,0:T(8,128)}), f32[128,2048]{1,0:T(8,128)}) %reduce-scatter.5.cloned.1.call-update) | async-done | bytes 1048592 | tf_op jit(solution)/shard_map/reduce_scatter | solution.py:44
  867.7 2.6 multiply_convert_fusion
  (7 shorter events, 0.0 us)
Async XLA Ops:
  6.5 51.8 %all-gather.2.cloned.1.call-start = ((), (), s32[]{:S(2)}) async-start(), calls=%async_computation.5 | async-start | bytes 2359296 | tf_op jit(solution)/shard_map/all_gather | solution.py:19
  8.4 52.7 %copy-start.1 = (f32[8192]{0:T(1024)S(1)}, f32[8192]{0:T(1024)}, u32[]{:S(2)}) copy-start(f32[8192]{0:T(1024)} %param.7) | copy-start | bytes 98308
  72.1 366.0 %all-to-all-start.1 = ((bf16[512,8,2048]{0,2,1:T(8,128)(2,1)}), bf16[512,8,2048]{0,2,1:T(8,128)(2,1)}, u32[]{:S(2)}, u32[]{:S(2)}) async-start(bf16[512,8,2048]{0,2,1:T(8,128)(2,1)} %bitcast.20), calls=%async_computation.1 | async-start | bytes 33554432 | tf_op jit(solution)/shard_map/all_to_all | solution.py:30
  438.1 367.5 %all-to-all-start.2 = ((bf16[512,8,2048]{0,2,1:T(8,128)(2,1)}), bf16[512,8,2048]{0,2,1:T(8,128)(2,1)}, u32[]{:S(2)}, u32[]{:S(2)}) async-start(bf16[512,8,2048]{0,2,1:T(8,128)(2,1)} %bitcast.19), calls=%async_computation.3 | async-start | bytes 33554432 | tf_op jit(solution)/shard_map/all_to_all | solution.py:31
  446.8 407.1 %reduce-scatter.3.cloned.1.call-start = ((), (), s32[]{:S(2)}) async-start(), calls=%async_computation.6 | async-start | bytes 3145728 | tf_op jit(solution)/shard_map/reduce_scatter | solution.py:43
  624.9 21.8 %copy-start = (bf16[2,128,4096]{2,1,0:T(8,128)(2,1)S(1)}, bf16[2,128,4096]{2,1,0:T(8,128)(2,1)}, u32[]{:S(2)}) copy-start(bf16[2,128,4096]{2,1,0:T(8,128)(2,1)} %copy.8) | copy-start | bytes 6291460
  656.1 211.6 %reduce-scatter.5.cloned.1.call-start = ((), (), s32[]{:S(2)}) async-start(), calls=%async_computation.7 | async-start | bytes 3145728 | tf_op jit(solution)/shard_map/reduce_scatter | solution.py:44
Sparse Core Ops, SparseCore 0:
  9.5 48.8 all-gather.1
  656.3 12.1 reduce-scatter.2
  854.0 13.6 reduce-scatter.4
where the time goes:
time: 884 us; the launch traced here: 877 us
  waiting for transfers between devices  528 us (60%)
  local copies, waits for them, and re-layouts  250 us (28%)
  other arithmetic  45.1 us (5%)
  matrix products  18.9 us (2%)
  starting transfers between devices  15.4 us (2%)
  between operations  13.1 us (1%)
    all_to_all x1, waiting for transfers between devices, local(): lax.all_to_all(gate_weight, 'tensor', split_axis=1, concat_axis=0, tiled=...  337 us
    mul x8, local copies, waits for them, and re-layouts, apply_mask(): blocks = blocks * mask.astype(jnp.bfloat16)[:, None, :, None]  201 us
    all_to_all x1, waiting for transfers between devices, local(): lax.all_to_all(up_weight, 'tensor', split_axis=1, concat_axis=0, tiled=True)  149 us
    unnamed x7, local copies, waits for them, and re-layouts  46.7 us
    mul x2, other arithmetic, apply_mask(): blocks = blocks * mask.astype(jnp.bfloat16)[:, None, :, None]  34.3 us
    all_gather x1, waiting for transfers between devices, local(): whole = lax.all_gather(tokens, 'tensor', axis=1, tiled=True)  27.6 us
  transfers between devices with their start and end apart: 5, of which 4 were waited for; matrix products, arithmetic and copies ran while one was open for 34% of the time, Pallas kernels for 0%

commit v1 on v0

v1 whole, which is shorter than its diff:
```python
import functools

import jax
import jax.numpy as jnp
from jax import lax
from jax.experimental import pallas as pl
from jax.experimental.pallas import tpu as pltpu
from jax.sharding import PartitionSpec as P

BS = 64
SUB = 512
LAG = 6
W_SLOTS = 4
X_SLOTS = 4
EPS = 1e-05
MESH = pl.DeviceIdType.MESH


def kernel(
    nt, ny, sub, tok_ref, gain_ref, gw_hbm, uw_hbm, gm_ref, um_ref, out_ref,
    stats, stat_out, xbuf, xs, mexp, wbuf, own, xsend, xrecv, ysend, yrecv, zsend, zrecv,
    stat_ssem, stat_rsem, tok_ssem, tok_rsem, wsem, x_ssem, x_rsem, y_ssem, y_rsem, z_ssem, z_rsem,
):
    nz = nt // ny
    w = lax.axis_index("wide")
    t = lax.axis_index("tensor")
    z, y = lax.div(t, ny), lax.rem(t, ny)
    me = w * nt + t
    peers = 2 * nt
    rows, feats = tok_ref.shape
    depth, ff = gw_hbm.shape
    width = ff // nt
    per = width // sub
    pairs = nz * per
    units = 2 * pairs
    blocks = depth // BS

    def at(dev):
        return {"wide": lax.div(dev, nt), "tensor": lax.rem(dev, nt)}

    def z_of(pair):
        k = lax.div(pair, per)
        right, left = nz - 1 - z, z
        both = jnp.minimum(right, left)
        paired = k < 2 * both
        idx = jnp.where(paired, lax.div(k, 2), k - both)
        is_right = jnp.where(paired, lax.rem(k, 2) == 0, right > left)
        dest = jnp.where(is_right, nz - 1 - idx, idx)
        return jnp.where(k == nz - 1, z, dest)

    def column(unit):
        pair, kind = lax.div(unit, 2), lax.rem(unit, 2)
        y_to = jnp.where(kind == 0, ny - 1 - y, y)
        owner = z_of(pair) * ny + y_to
        return pl.multiple_of(owner * width + lax.rem(pair, per) * sub, 128)

    def weight_copies(unit):
        slot = lax.rem(unit, W_SLOTS)
        cols = pl.ds(column(unit), sub)
        return (
            pltpu.make_async_copy(gw_hbm.at[:, cols], wbuf.at[slot, 0], wsem.at[slot, 0]),
            pltpu.make_async_copy(uw_hbm.at[:, cols], wbuf.at[slot, 1], wsem.at[slot, 1]),
        )

    def fetch(unit):
        for copy in weight_copies(unit):
            copy.start()

    for unit in range(min(W_SLOTS, units)):
        fetch(jnp.int32(unit))

    barrier = pltpu.get_barrier_semaphore()

    @pl.loop(1, peers)
    def _(d):
        pl.semaphore_signal(
            barrier, inc=1, device_id=at(lax.rem(me + d, peers)), device_id_type=MESH
        )

    total = jnp.zeros((rows, 128), jnp.float32)
    for f in range(0, feats, 128):
        v = tok_ref[:, f:f + 128].astype(jnp.float32)
        total = total + v * v
    line = jnp.sum(total.T, axis=0, keepdims=True)
    stat_out[...] = jnp.broadcast_to(line, (8, rows))
    stats[me] = jnp.broadcast_to(line, (8, rows))

    pl.semaphore_wait(barrier, peers - 1)

    def token_copy(h):
        dev = 2 * t + h
        return dev, pltpu.make_async_remote_copy(
            src_ref=tok_ref.at[:, h * depth:(h + 1) * depth],
            dst_ref=xbuf.at[w],
            send_sem=tok_ssem.at[h],
            recv_sem=tok_rsem.at[w],
            device_id=at(dev),
            device_id_type=MESH,
        )

    for h in range(2):
        dev, copy = token_copy(h)

        @pl.when(dev != me)
        def _():
            copy.start()

        @pl.when(dev == me)
        def _():
            xbuf[w] = tok_ref[:, h * depth:(h + 1) * depth]

    def stat_copy(d, src):
        return pltpu.make_async_remote_copy(
            src_ref=stat_out,
            dst_ref=stats.at[src],
            send_sem=stat_ssem.at[d],
            recv_sem=stat_rsem.at[src],
            device_id=at(lax.rem(me + d, peers)),
            device_id_type=MESH,
        )

    @pl.loop(1, peers)
    def _(d):
        stat_copy(d, me).start()

    mrows = gm_ref.shape[0]
    pick = (
        lax.broadcasted_iota(jnp.int32, (8, mrows), 1)
        == lax.broadcasted_iota(jnp.int32, (8, mrows), 0) + me * blocks
    ).astype(jnp.float32).astype(jnp.bfloat16)
    mine = []
    for m_ref in (gm_ref, um_ref):
        kept = m_ref[...].astype(jnp.float32).astype(jnp.bfloat16)
        mine.append(
            jnp.dot(pick, kept, preferred_element_type=jnp.float32).astype(jnp.bfloat16)
        )
    mcols = gm_ref.shape[1]

    @pl.loop(0, ff // sub)
    def _(n):
        first = lax.broadcasted_iota(jnp.int32, (mcols, sub), 0) * BS - n * sub
        col = lax.broadcasted_iota(jnp.int32, (mcols, sub), 1)
        spread = ((col >= first) & (col < first + BS)).astype(jnp.float32).astype(jnp.bfloat16)
        for a in range(2):
            mexp[a, :, pl.ds(pl.multiple_of(n * sub, 128), sub)] = jnp.dot(
                mine[a], spread, preferred_element_type=jnp.float32
            )

    @pl.loop(1, peers)
    def _(d):
        stat_copy(d, lax.rem(me + d, peers)).wait_recv()

    for v in range(2):
        @pl.when(v * nt + lax.div(me, 2) != me)
        def _():
            pltpu.make_async_remote_copy(
                src_ref=tok_ref.at[:, 0:depth], dst_ref=xbuf.at[v],
                send_sem=tok_ssem.at[0], recv_sem=tok_rsem.at[v],
                device_id=at(lax.rem(me + 1, peers)), device_id_type=MESH,
            ).wait_recv()

    gain = gain_ref[:, pl.ds(pl.multiple_of(me * depth, 128), depth)]
    for half in range(2):
        v = w if half == 0 else 1 - w
        ssq = jnp.sum(stats[pl.ds(v * nt, nt)], axis=0)[0:1, :]
        scale = lax.rsqrt(ssq / (feats * nt) + EPS)
        scale = jnp.broadcast_to(scale, (rows, rows)).T[:, 0:1]
        xs[half * rows:(half + 1) * rows, :] = (
            xbuf[v].astype(jnp.float32) * scale * gain
        ).astype(jnp.bfloat16)

    def x_copy(unit):
        slot = lax.rem(unit, X_SLOTS)
        return pltpu.make_async_remote_copy(
            src_ref=xsend.at[slot], dst_ref=xrecv.at[unit],
            send_sem=x_ssem.at[slot], recv_sem=x_rsem.at[unit],
            device_id={"wide": 1 - w}, device_id_type=MESH,
        )

    def y_copy(pair):
        return pltpu.make_async_remote_copy(
            src_ref=ysend.at[pair], dst_ref=yrecv.at[pair],
            send_sem=y_ssem.at[pair], recv_sem=y_rsem.at[pair],
            device_id={"tensor": z * ny + (ny - 1 - y)}, device_id_type=MESH,
        )

    def z_copy(pair, side, piece, z_to):
        return pltpu.make_async_remote_copy(
            src_ref=zsend.at[pair], dst_ref=zrecv.at[side, piece],
            send_sem=z_ssem.at[pair], recv_sem=z_rsem.at[side, piece],
            device_id={"tensor": z_to * ny + y}, device_id_type=MESH,
        )

    def compute(unit):
        slot = lax.rem(unit, W_SLOTS)
        xslot = lax.rem(unit, X_SLOTS)
        cols = pl.ds(column(unit), sub)
        for copy in weight_copies(unit):
            copy.wait()

        @pl.when(unit >= X_SLOTS)
        def _():
            x_copy(unit - X_SLOTS).wait_send()

        for a in range(2):
            kept = []
            for r in range(blocks):
                keep = jnp.broadcast_to(mexp[a, r:r + 1, cols], (BS, sub)).astype(jnp.bfloat16)
                kept.append(wbuf[slot, a, r * BS:(r + 1) * BS, :] * keep)
            part = jnp.dot(
                xs[...], jnp.concatenate(kept, axis=0), preferred_element_type=jnp.float32
            )
            own[xslot, :, a * sub:(a + 1) * sub] = part[:rows]
            xsend[xslot, :, a * sub:(a + 1) * sub] = part[rows:]
        x_copy(unit).start()

        @pl.when(unit + W_SLOTS < units)
        def _():
            fetch(unit + W_SLOTS)

    def finish(unit, kind):
        pair = lax.div(unit, 2)
        x_copy(unit).wait_recv()
        both = own[lax.rem(unit, X_SLOTS)] + xrecv[unit]
        if kind == 0:
            ysend[pair] = both.astype(jnp.bfloat16)
            y_copy(pair).start()
        else:
            xrecv[unit] = both

    def settle(pair):
        unit = 2 * pair + 1
        dest = z_of(pair)
        piece = dest * per + lax.rem(pair, per)
        y_copy(pair).wait_recv()
        xrecv[unit] = xrecv[unit] + yrecv[pair].astype(jnp.float32)

        @pl.when((dest >= z) & (z > 0))
        def _():
            z_copy(pair, 0, piece, z - 1).wait_recv()
            xrecv[unit] = xrecv[unit] + zrecv[0, piece].astype(jnp.float32)

        @pl.when((dest <= z) & (z < nz - 1))
        def _():
            z_copy(pair, 1, piece, z + 1).wait_recv()
            xrecv[unit] = xrecv[unit] + zrecv[1, piece].astype(jnp.float32)

        @pl.when(dest != z)
        def _():
            zsend[pair] = xrecv[unit].astype(jnp.bfloat16)

        @pl.when(dest > z)
        def _():
            z_copy(pair, 0, piece, z + 1).start()

        @pl.when(dest < z)
        def _():
            z_copy(pair, 1, piece, z - 1).start()

        @pl.when(dest == z)
        def _():
            g = xrecv[unit, :, 0:sub]
            u = xrecv[unit, :, sub:2 * sub]
            at_col = pl.multiple_of(lax.rem(pair, per) * sub, 128)
            out_ref[:, pl.ds(at_col, sub)] = (g / (1.0 + jnp.exp(-g)) * u).astype(out_ref.dtype)

    @pl.loop(0, pairs + LAG)
    def _(i):
        @pl.when(i < pairs)
        def _():
            compute(2 * i)

        @pl.when((i >= 1) & (i <= pairs))
        def _():
            finish(2 * i - 1, 1)

        @pl.when(i < pairs)
        def _():
            compute(2 * i + 1)
            finish(2 * i, 0)

        @pl.when(i >= LAG)
        def _():
            settle(i - LAG)

    for unit in range(max(0, units - X_SLOTS), units):
        x_copy(jnp.int32(unit)).wait_send()

    @pl.loop(0, pairs)
    def _(pair):
        y_copy(pair).wait_send()

        @pl.when(z_of(pair) != z)
        def _():
            z_copy(pair, 0, pair, lax.rem(z + 1, nz)).wait_send()

    @pl.loop(1, peers)
    def _(d):
        stat_copy(d, me).wait_send()

    for h in range(2):
        dev, copy = token_copy(h)

        @pl.when(dev != me)
        def _():
            copy.wait_send()


def local(tokens, gain, gate_weight, up_weight, gate_mask, up_mask):
    nt = lax.axis_size("tensor")
    ny = 2
    rows, feats = tokens.shape
    depth, ff = gate_weight.shape
    width = ff // nt
    sub = min(SUB, width)
    pairs = (nt // ny) * (width // sub)
    peers = 2 * nt
    dma = pltpu.SemaphoreType.DMA
    vmem = pl.BlockSpec(memory_space=pltpu.VMEM)
    hbm = pl.BlockSpec(memory_space=pl.ANY)
    tile = (rows, 2 * sub)
    return pl.pallas_call(
        functools.partial(kernel, nt, ny, sub),
        out_shape=jax.ShapeDtypeStruct((rows, width), jnp.bfloat16),
        in_specs=[vmem, vmem, hbm, hbm, vmem, vmem],
        out_specs=vmem,
        scratch_shapes=[
            pltpu.VMEM((peers, 8, rows), jnp.float32),
            pltpu.VMEM((8, rows), jnp.float32),
            pltpu.VMEM((2, rows, depth), jnp.bfloat16),
            pltpu.VMEM((2 * rows, depth), jnp.bfloat16),
            pltpu.VMEM((2, 8, ff), jnp.float32),
            pltpu.VMEM((W_SLOTS, 2, depth, sub), jnp.bfloat16),
            pltpu.VMEM((X_SLOTS,) + tile, jnp.float32),
            pltpu.VMEM((X_SLOTS,) + tile, jnp.float32),
            pltpu.VMEM((2 * pairs,) + tile, jnp.float32),
            pltpu.VMEM((pairs,) + tile, jnp.bfloat16),
            pltpu.VMEM((pairs,) + tile, jnp.bfloat16),
            pltpu.VMEM((pairs,) + tile, jnp.bfloat16),
            pltpu.VMEM((2, pairs) + tile, jnp.bfloat16),
            dma((peers,)), dma((peers,)), dma((2,)), dma((2,)), dma((W_SLOTS, 2)),
            dma((X_SLOTS,)), dma((2 * pairs,)), dma((pairs,)), dma((pairs,)),
            dma((pairs,)), dma((2, pairs)),
        ],
        compiler_params=pltpu.CompilerParams(
            collective_id=0, has_side_effects=True, vmem_limit_bytes=60 * 1024 * 1024
        ),
    )(tokens, gain.reshape(1, -1), gate_weight, up_weight, gate_mask, up_mask)


def solution(mesh):
    in_specs = (
        P(("group", "wide"), "tensor"),
        P("group"),
        P(("group", "wide", "tensor"), None),
        P(("group", "wide", "tensor"), None),
        P("group", None),
        P("group", None),
    )
    out_specs = P(("group", "wide"), "tensor")
    return jax.shard_map(local, mesh=mesh, in_specs=in_specs, out_specs=out_specs, check_vma=False)
```

time: 884 us -> 121 us (0.14)
  waiting for transfers between devices: 528 us -> 0 us
  local copies, waits for them, and re-layouts: 250 us -> 1.88 us
  Pallas kernels: 0 us -> 119 us
  other arithmetic: 45.1 us -> 0 us
  matrix products: 18.9 us -> 0 us
  starting transfers between devices: 15.4 us -> 0 us
  between operations: 13.1 us -> 0.01 us
    all_to_all x2 -> x0, waiting for transfers between devices: 486 us -> none  [the longest x1 337 us: local(): lax.all_to_all(gate_weight, 'tensor', split_axis=1, concat_axis=0, tiled=...]
    mul x8 -> x0, local copies, waits for them, and re-layouts: 201 us -> none  [apply_mask(): blocks = blocks * mask.astype(jnp.bfloat16)[:, None, :, None]]
    pallas_call x0 -> x1, Pallas kernels: none -> 119 us  [local(): pl.pallas_call(functools.partial(kernel, nt, ny, sub), out_shape=jax.Shap...]
    unnamed x7 -> x1, local copies, waits for them, and re-layouts: 46.7 us -> 1.88 us
    mul x2 -> x0, other arithmetic: 34.3 us -> none  [apply_mask(): blocks = blocks * mask.astype(jnp.bfloat16)[:, None, :, None]]
    all_gather x1 -> x0, waiting for transfers between devices: 27.6 us -> none  [local(): whole = lax.all_gather(tokens, 'tensor', axis=1, tiled=True)]
    dot_general x2 -> x0, matrix products: 18.9 us -> none  [the longest x1 9.46 us: local(): jnp.dot(features_half, up_kept, preferred_element_type=jnp.float32)]
    all_to_all x2 -> x0, starting transfers between devices: 15.1 us -> none  [the longest x1 8.74 us: local(): lax.all_to_all(up_weight, 'tensor', split_axis=1, concat_axis=0, tiled=True)]
  transfers between devices with their start and end apart: 5 -> 0, of which waited for: 4 -> 0; matrix products, arithmetic and copies ran while one was open for 34% -> 0% of each run, Pallas kernels for 0% -> 0%
where the time goes in v1:
time: 121 us
  Pallas kernels  119 us (98%)
  local copies, waits for them, and re-layouts  1.88 us (2%)
    pallas_call x1, Pallas kernels, local(): pl.pallas_call(functools.partial(kernel, nt, ny, sub), out_shape=jax.Shap...  119 us

profile of v1, /device:TPU:17, one launch (start us, length us, event | category | flops | bytes accessed | tf_op | source)
XLA Modules:
  0.0 121.2 jit_solution(9505412799958524423)
XLA Ops:
  0.0 119.3 %shard_map.64 = bf16[128,2048]{1,0:T(8,128)(2,1)} custom-call(bf16[128,1024]{1,0:T(8,128)(2,1)} %tok_ref.1, f32[1,8192]{1,0:T(1,128)} %bitcast.1, bf16[512,16384]{1,0:T(8,128)(2,1)} %gw_hbm.1, bf16[512,16384]{1,0:T(8,128)(2,1)} %uw_hbm.1, s32[128,256]{1,0:T(8,128)} %gm_ref.1, s32[128,256]{1,0:T(8,128)} %um_ref.1), custom_call_target="tpu_custom_call" | custom-call | tf_op jit(solution)/shard_map/pallas_call | solution.py:322
  119.3 1.9 %copy.8 = bf16[128,2048]{1,0:T(8,128)(2,1)} copy(bf16[128,2048]{1,0:T(8,128)(2,1)} %shard_map.64) | data formatting | bytes 1048576

commit v2 on v1

--- a/solution.py
+++ b/solution.py
@@ -18,7 +18,7 @@
 
 def kernel(
     nt, ny, sub, tok_ref, gain_ref, gw_hbm, uw_hbm, gm_ref, um_ref, out_ref,
-    stats, stat_out, xbuf, xs, mexp, wbuf, own, xsend, xrecv, ysend, yrecv, zsend, zrecv,
+    stats, stat_out, xbuf, xs, mine, wbuf, own, xsend, xrecv, ysend, yrecv, zsend, zrecv,
     stat_ssem, stat_rsem, tok_ssem, tok_rsem, wsem, x_ssem, x_rsem, y_ssem, y_rsem, z_ssem, z_rsem,
 ):
     nz = nt // ny
@@ -44,7 +44,7 @@
         both = jnp.minimum(right, left)
         paired = k < 2 * both
         idx = jnp.where(paired, lax.div(k, 2), k - both)
-        is_right = jnp.where(paired, lax.rem(k, 2) == 0, right > left)
+        is_right = jnp.where(paired, (lax.rem(k, 2) == 0) == (right > left), right > left)
         dest = jnp.where(is_right, nz - 1 - idx, idx)
         return jnp.where(k == nz - 1, z, dest)
 
@@ -128,23 +128,10 @@
         lax.broadcasted_iota(jnp.int32, (8, mrows), 1)
         == lax.broadcasted_iota(jnp.int32, (8, mrows), 0) + me * blocks
     ).astype(jnp.float32).astype(jnp.bfloat16)
-    mine = []
-    for m_ref in (gm_ref, um_ref):
+    for a, m_ref in enumerate((gm_ref, um_ref)):
         kept = m_ref[...].astype(jnp.float32).astype(jnp.bfloat16)
-        mine.append(
-            jnp.dot(pick, kept, preferred_element_type=jnp.float32).astype(jnp.bfloat16)
-        )
+        mine[a * 8:(a + 1) * 8, :] = jnp.dot(pick, kept, preferred_element_type=jnp.float32)
     mcols = gm_ref.shape[1]
-
-    @pl.loop(0, ff // sub)
-    def _(n):
-        first = lax.broadcasted_iota(jnp.int32, (mcols, sub), 0) * BS - n * sub
-        col = lax.broadcasted_iota(jnp.int32, (mcols, sub), 1)
-        spread = ((col >= first) & (col < first + BS)).astype(jnp.float32).astype(jnp.bfloat16)
-        for a in range(2):
-            mexp[a, :, pl.ds(pl.multiple_of(n * sub, 128), sub)] = jnp.dot(
-                mine[a], spread, preferred_element_type=jnp.float32
-            )
 
     @pl.loop(1, peers)
     def _(d):
@@ -194,7 +181,10 @@
     def compute(unit):
         slot = lax.rem(unit, W_SLOTS)
         xslot = lax.rem(unit, X_SLOTS)
-        cols = pl.ds(column(unit), sub)
+        first = lax.broadcasted_iota(jnp.int32, (mcols, sub), 0) * BS - column(unit)
+        col = lax.broadcasted_iota(jnp.int32, (mcols, sub), 1)
+        spread = ((col >= first) & (col < first + BS)).astype(jnp.float32).astype(jnp.bfloat16)
+        mexp = jnp.dot(mine[...].astype(jnp.bfloat16), spread, preferred_element_type=jnp.float32)
         for copy in weight_copies(unit):
             copy.wait()
 
@@ -205,7 +195,7 @@
         for a in range(2):
             kept = []
             for r in range(blocks):
-                keep = jnp.broadcast_to(mexp[a, r:r + 1, cols], (BS, sub)).astype(jnp.bfloat16)
+                keep = jnp.broadcast_to(mexp[a * 8 + r:a * 8 + r + 1, :], (BS, sub)).astype(jnp.bfloat16)
                 kept.append(wbuf[slot, a, r * BS:(r + 1) * BS, :] * keep)
             part = jnp.dot(
                 xs[...], jnp.concatenate(kept, axis=0), preferred_element_type=jnp.float32
@@ -276,8 +266,8 @@
 
         @pl.when(i < pairs)
         def _():
+            finish(2 * i, 0)
             compute(2 * i + 1)
-            finish(2 * i, 0)
 
         @pl.when(i >= LAG)
         def _():
@@ -329,7 +319,7 @@
             pltpu.VMEM((8, rows), jnp.float32),
             pltpu.VMEM((2, rows, depth), jnp.bfloat16),
             pltpu.VMEM((2 * rows, depth), jnp.bfloat16),
-            pltpu.VMEM((2, 8, ff), jnp.float32),
+            pltpu.VMEM((16, gate_mask.shape[1]), jnp.float32),
             pltpu.VMEM((W_SLOTS, 2, depth, sub), jnp.bfloat16),
             pltpu.VMEM((X_SLOTS,) + tile, jnp.float32),
             pltpu.VMEM((X_SLOTS,) + tile, jnp.float32),

time: 121 us -> 116 us (0.959); the launches traced: 121 us -> 114 us
  Pallas kernels: 119 us -> 112 us
    pallas_call x1, Pallas kernels: 119 us -> 112 us  [local(): pl.pallas_call(functools.partial(kernel, nt, ny, sub), out_shape=jax.Shap...]
where the time goes in v2:
time: 116 us; the launch traced here: 114 us
  Pallas kernels  112 us (97%)
  local copies, waits for them, and re-layouts  1.88 us (2%)
    pallas_call x1, Pallas kernels, local(): pl.pallas_call(functools.partial(kernel, nt, ny, sub), out_shape=jax.Shap...  112 us

profile of v2, /device:TPU:17, one launch (start us, length us, event | category | flops | bytes accessed | tf_op | source)
XLA Modules:
  0.0 113.8 jit_solution(16908139256841428027)
XLA Ops:
  0.0 111.9 %shard_map.64 = bf16[128,2048]{1,0:T(8,128)(2,1)} custom-call(bf16[128,1024]{1,0:T(8,128)(2,1)} %tok_ref.1, f32[1,8192]{1,0:T(1,128)} %bitcast.1, bf16[512,16384]{1,0:T(8,128)(2,1)} %gw_hbm.1, bf16[512,16384]{1,0:T(8,128)(2,1)} %uw_hbm.1, s32[128,256]{1,0:T(8,128)} %gm_ref.1, s32[128,256]{1,0:T(8,128)} %um_ref.1), custom_call_target="tpu_custom_call" | custom-call | tf_op jit(solution)/shard_map/pallas_call | solution.py:312
  111.9 1.9 %copy.8 = bf16[128,2048]{1,0:T(8,128)(2,1)} copy(bf16[128,2048]{1,0:T(8,128)(2,1)} %shard_map.64) | data formatting | bytes 1048576
